TPU v7x, 256 devices: a whole 4x4x8 slice. The times are simulated.
256 devices in a mesh: dp: 16 (over x, y_hi, core), fsdp: 16 (over y_lo, z).
Axes of the slice: x: 4, y: 4 (y_hi: 2, y_lo: 2; y = y_hi * 2 + y_lo), z: 8, core: 2. Of those that a mesh axis runs over, the one named last changes fastest.
Arguments:
- tokens: bfloat16 [8192, 2048], P('dp'), may hold values from -6 to 6
- expert_ids: int32 [8192, 2], P('dp'), may hold values from 0 to 7, as said below
- route_probs: float32 [8192, 2], P('dp'), may hold values from 0.1 to 1
- gate_w: bfloat16 [2, 2048, 7168], P(None, 'dp', 'fsdp'), may hold values from -0.125 to 0.125
- up_w: bfloat16 [2, 2048, 7168], P(None, 'dp', 'fsdp'), may hold values from -0.125 to 0.125
- down_w: bfloat16 [2, 7168, 2048], P(None, 'fsdp', 'dp'), may hold values from -0.0625 to 0.0625
- out_grad: bfloat16 [8192, 2048], P('dp'), may hold values from -6 to 6
Outputs:
- mixed: bfloat16 [8192, 2048], P('dp')
- token_grad: bfloat16 [8192, 2048], P('dp')
- gate_grad: bfloat16 [2, 2048, 7168], P(None, 'dp', 'fsdp')
- up_grad: bfloat16 [2, 2048, 7168], P(None, 'dp', 'fsdp')
- down_grad: bfloat16 [2, 7168, 2048], P(None, 'fsdp', 'dp')
Inputs may be any that keep to these rules, and one draw needn't show every extreme that they name: `expert_ids`: the two entries of a row differ. In each aligned block of 512 rows (the rows of one index of dp) every expert is named by at most 256 rows, and one of experts 0 to 1 by exactly 256 rows.
All inputs are finite; a program needn't handle non-finite values.
Results may differ from a plain program's by a relative error of at most 0.018.
Values may be sent and summed in bfloat16 or wider, within the bound.
A program may use at most 128 MiB of HBM per device.

v0:
```python
import jax
import jax.numpy as jnp
from jax import lax
from jax.sharding import PartitionSpec as P


def slot_layout(expert_ids, route_probs, expert, slot_cap):
    token_count = expert_ids.shape[0]
    matches = expert_ids == expert
    chosen = jnp.any(matches, axis=1)
    weight_token = jnp.sum(jnp.where(matches, route_probs, jnp.float32(0.0)), axis=1)
    position = jnp.cumsum(chosen.astype(jnp.int32)) - 1
    slot_index = lax.broadcasted_iota(jnp.int32, (slot_cap, token_count), 0)
    token_index = lax.broadcasted_iota(jnp.int32, (slot_cap, token_count), 1)
    matched_slots = (position[None, :] == slot_index) & chosen[None, :]
    slot_token = jnp.sum(jnp.where(matched_slots, token_index, 0), axis=1)
    slot_valid = jnp.any(matched_slots, axis=1)
    slot_weight = jnp.where(slot_valid, jnp.take(weight_token, slot_token), jnp.float32(0.0))
    token_slot = jnp.clip(position, 0, slot_cap - 1)
    return (chosen, token_slot, slot_token, slot_valid, slot_weight)


def group_total(partial_value):
    return lax.psum(partial_value.astype(jnp.bfloat16), "fsdp")


def body(tokens, expert_ids, route_probs, gate_w, up_w, down_w, out_grad):
    token_count = tokens.shape[0]
    width = tokens.shape[1]
    slot_cap = token_count // 2
    window = gate_w.shape[0]
    mixed_part = jnp.zeros((token_count, width), jnp.float32)
    stored = []
    for expert in range(window):
        chosen, token_slot, slot_token, slot_valid, slot_weight = slot_layout(
            expert_ids, route_probs, expert, slot_cap
        )
        gate_full, up_full, down_full = (
            lax.all_gather(gate_w[expert], "dp", axis=0, tiled=True),
            lax.all_gather(up_w[expert], "dp", axis=0, tiled=True),
            lax.all_gather(down_w[expert], "dp", axis=1, tiled=True),
        )
        slot_input = jnp.take(tokens, slot_token, axis=0) * slot_valid[:, None].astype(tokens.dtype)
        gate_act = jnp.dot(slot_input, gate_full, preferred_element_type=jnp.float32)
        up_act = jnp.dot(slot_input, up_full, preferred_element_type=jnp.float32)
        hidden = (jax.nn.silu(gate_act) * up_act).astype(jnp.bfloat16)
        expert_out = (
            jnp.dot(hidden, down_full, preferred_element_type=jnp.float32) * slot_weight[:, None]
        )
        mixed_part = mixed_part + jnp.where(
            chosen[:, None], jnp.take(expert_out, token_slot, axis=0), jnp.float32(0.0)
        )
        stored.append(
            (
                chosen,
                token_slot,
                slot_token,
                slot_weight,
                slot_input,
                gate_act,
                up_act,
                hidden,
                gate_full,
                up_full,
                down_full,
            )
        )
    mixed = group_total(mixed_part)
    grad_part = jnp.zeros((token_count, width), jnp.float32)
    gate_grads, up_grads, down_grads = ([], [], [])
    for expert in range(window):
        (
            chosen,
            token_slot,
            slot_token,
            slot_weight,
            slot_input,
            gate_act,
            up_act,
            hidden,
            gate_full,
            up_full,
            down_full,
        ) = stored[expert]
        slot_grad = (
            jnp.take(out_grad, slot_token, axis=0).astype(jnp.float32) * slot_weight[:, None]
        ).astype(jnp.bfloat16)
        down_term = lax.dot_general(
            hidden, slot_grad, (((0,), (0,)), ((), ())), preferred_element_type=jnp.float32
        )
        hidden_grad = lax.dot_general(
            slot_grad, down_full, (((1,), (1,)), ((), ())), preferred_element_type=jnp.float32
        )
        sigma = jax.nn.sigmoid(gate_act)
        up_act_grad = (hidden_grad * gate_act * sigma).astype(jnp.bfloat16)
        gate_act_grad = (hidden_grad * up_act * sigma * (1.0 + gate_act * (1.0 - sigma))).astype(
            jnp.bfloat16
        )
        gate_term = lax.dot_general(
            slot_input, gate_act_grad, (((0,), (0,)), ((), ())), preferred_element_type=jnp.float32
        )
        up_term = lax.dot_general(
            slot_input, up_act_grad, (((0,), (0,)), ((), ())), preferred_element_type=jnp.float32
        )
        input_grad = lax.dot_general(
            gate_act_grad, gate_full, (((1,), (1,)), ((), ())), preferred_element_type=jnp.float32
        )
        input_grad = input_grad + lax.dot_general(
            up_act_grad, up_full, (((1,), (1,)), ((), ())), preferred_element_type=jnp.float32
        )
        grad_part = grad_part + jnp.where(
            chosen[:, None], jnp.take(input_grad, token_slot, axis=0), jnp.float32(0.0)
        )
        gate_sum, up_sum, down_sum = (
            lax.psum_scatter(
                gate_term.astype(jnp.bfloat16), "dp", scatter_dimension=0, tiled=True
            ).astype(jnp.float32),
            lax.psum_scatter(
                up_term.astype(jnp.bfloat16), "dp", scatter_dimension=0, tiled=True
            ).astype(jnp.float32),
            lax.psum_scatter(
                down_term.astype(jnp.bfloat16), "dp", scatter_dimension=1, tiled=True
            ).astype(jnp.float32),
        )
        gate_grads.append(gate_sum.astype(jnp.bfloat16))
        up_grads.append(up_sum.astype(jnp.bfloat16))
        down_grads.append(down_sum.astype(jnp.bfloat16))
    gate_grad = jnp.stack(gate_grads)
    up_grad = jnp.stack(up_grads)
    down_grad = jnp.stack(down_grads)
    token_grad = group_total(grad_part)
    return (mixed, token_grad, gate_grad, up_grad, down_grad)


def solution(mesh):
    placed = (
        P("dp", None),
        P("dp", None),
        P("dp", None),
        P(None, "dp", "fsdp"),
        P(None, "dp", "fsdp"),
        P(None, "fsdp", "dp"),
        P("dp", None),
    )
    return jax.shard_map(
        body,
        mesh=mesh,
        in_specs=placed,
        out_specs=(
            P("dp", None),
            P("dp", None),
            P(None, "dp", "fsdp"),
            P(None, "dp", "fsdp"),
            P(None, "fsdp", "dp"),
        ),
        check_vma=False,
    )
```

profile of v0, /device:TPU:4, one launch (start us, length us, event | category | flops | bytes accessed | tf_op | source)
XLA Modules:
  0.0 1003.4 jit_solution(5504983384310768062)
XLA Ops:
  7.2 1.8 fusion.32
  9.1 1.7 fusion.31
  10.8 1.7 fusion.30
  16.1 1.9 gather_fusion.4
  18.1 1.4 gather_fusion.3
  19.5 5.2 gather_fusion.8
  24.7 41.6 %all-gather.21.cloned.1.call-done = bf16[1,2048,448]{1,2,0:T(8,128)(2,1)} async-done(((bf16[1,128,448]{1,2,0:T(8,128)(2,1)}), bf16[1,2048,448]{1,2,0:T(8,128)(2,1)}) %all-gather.21.cloned.1.call-update) | async-done | bytes 1835024 | tf_op jit(solution)/shard_map/all_gather | solution.py:40
  66.2 3.1 fusion.8
  69.3 52.5 %all-gather.19.cloned.1.call-done = bf16[1,2048,448]{1,2,0:T(8,128)(2,1)} async-done(((bf16[1,128,448]{1,2,0:T(8,128)(2,1)}), bf16[1,2048,448]{1,2,0:T(8,128)(2,1)}) %all-gather.19.cloned.1.call-update) | async-done | bytes 1835024 | tf_op jit(solution)/shard_map/all_gather | solution.py:39
  121.8 3.0 fusion.12
  124.9 52.0 %all-gather.23.cloned.1.call-done = bf16[1,448,2048]{2,1,0:T(8,128)(2,1)} async-done(((bf16[1,448,128]{2,1,0:T(8,128)(2,1)}), bf16[1,448,2048]{2,1,0:T(8,128)(2,1)}) %all-gather.23.cloned.1.call-update) | async-done | bytes 1835024 | tf_op jit(solution)/shard_map/all_gather | solution.py:41
  176.9 3.7 multiply_convert_fusion.2
  180.5 0.7 copy-done.10
  181.2 2.0 convolution_convert_fusion.4
  183.2 3.8 copy.22
  187.3 2.3 gather_fusion
  189.6 4.3 gather_fusion.6
  194.1 1.9 gather_fusion.1
  196.1 36.2 %all-gather.15.cloned.1.call-done = bf16[1,2048,448]{1,2,0:T(8,128)(2,1)} async-done(((bf16[1,128,448]{1,2,0:T(8,128)(2,1)}), bf16[1,2048,448]{1,2,0:T(8,128)(2,1)}) %all-gather.15.cloned.1.call-update) | async-done | bytes 1835024 | tf_op jit(solution)/shard_map/all_gather | solution.py:40
  232.3 3.0 fusion.18
  235.4 52.4 %all-gather.13.cloned.1.call-done = bf16[1,2048,448]{1,2,0:T(8,128)(2,1)} async-done(((bf16[1,128,448]{1,2,0:T(8,128)(2,1)}), bf16[1,2048,448]{1,2,0:T(8,128)(2,1)}) %all-gather.13.cloned.1.call-update) | async-done | bytes 1835024 | tf_op jit(solution)/shard_map/all_gather | solution.py:39
  287.8 3.1 fusion.22
  290.9 51.8 %all-gather.17.cloned.1.call-done = bf16[1,448,2048]{2,1,0:T(8,128)(2,1)} async-done(((bf16[1,448,128]{2,1,0:T(8,128)(2,1)}), bf16[1,448,2048]{2,1,0:T(8,128)(2,1)}) %all-gather.17.cloned.1.call-update) | async-done | bytes 1835024 | tf_op jit(solution)/shard_map/all_gather | solution.py:41
  342.7 3.3 multiply_convert_fusion.4
  346.0 0.7 copy-done.16
  346.7 2.0 convolution_convert_fusion.5
  348.7 2.4 copy.20
  351.2 2.0 convolution_convert_fusion.1
  353.2 2.5 copy.16
  355.8 2.0 convolution_convert_fusion.3
  357.8 2.4 copy.12
  360.3 0.8 convolution_convert_fusion
  361.1 2.5 copy.18
  363.7 0.8 convolution_convert_fusion.2
  364.5 2.4 copy.14
  367.2 2.3 convolution_multiply_fusion.1
  369.5 3.6 gather_fusion.2
  373.1 2.4 fusion.20
  375.5 0.7 convolution_add_fusion.1
  376.3 3.6 gather_fusion.7
  379.9 2.2 convolution_multiply_fusion
  382.2 3.6 gather_fusion.5
  385.8 2.4 fusion.10
  388.1 0.7 convolution_add_fusion
  388.9 3.6 gather_fusion.9
  392.4 9.4 fusion.1
  401.9 22.4 %reduce-scatter.29.cloned.1.call-done = bf16[128,448]{1,0:T(8,128)(2,1)} async-done(((bf16[2048,448]{1,0:T(8,128)(2,1)}), bf16[128,448]{1,0:T(8,128)(2,1)}) %reduce-scatter.29.cloned.1.call-update) | async-done | bytes 114704
  424.3 1.0 copy.23
  425.3 80.9 %reduce-scatter.27.cloned.1.call-done = bf16[128,448]{1,0:T(8,128)(2,1)} async-done(((bf16[2048,448]{1,0:T(8,128)(2,1)}), bf16[128,448]{1,0:T(8,128)(2,1)}) %reduce-scatter.27.cloned.1.call-update) | async-done | bytes 114704
  506.3 1.0 copy.21
  507.3 80.9 %reduce-scatter.23.cloned.1.call-done = bf16[128,448]{1,0:T(8,128)(2,1)} async-done(((bf16[2048,448]{1,0:T(8,128)(2,1)}), bf16[128,448]{1,0:T(8,128)(2,1)}) %reduce-scatter.23.cloned.1.call-update) | async-done | bytes 114704
  588.3 1.0 copy.17
  589.3 80.8 %reduce-scatter.19.cloned.1.call-done = bf16[128,448]{1,0:T(8,128)(2,1)} async-done(((bf16[2048,448]{1,0:T(8,128)(2,1)}), bf16[128,448]{1,0:T(8,128)(2,1)}) %reduce-scatter.19.cloned.1.call-update) | async-done | bytes 114704
  670.1 1.0 copy.13
  671.1 81.0 %reduce-scatter.25.cloned.1.call-done = bf16[128,448]{1,0:T(8,128)(2,1)} async-done(((bf16[2048,448]{1,0:T(8,128)(2,1)}), bf16[128,448]{1,0:T(8,128)(2,1)}) %reduce-scatter.25.cloned.1.call-update) | async-done | bytes 114704
  752.1 1.0 copy.19
  753.1 80.8 %reduce-scatter.21.cloned.1.call-done = bf16[128,448]{1,0:T(8,128)(2,1)} async-done(((bf16[2048,448]{1,0:T(8,128)(2,1)}), bf16[128,448]{1,0:T(8,128)(2,1)}) %reduce-scatter.21.cloned.1.call-update) | async-done | bytes 114704
  833.9 1.0 copy.15
  835.0 0.7 pad_maximum_fusion.2
  835.7 0.7 pad_maximum_fusion.1
  836.4 0.7 pad_maximum_fusion
  837.1 155.1 %all-reduce.3.cloned.1.call-done = (bf16[512,2048]{1,0:T(8,128)(2,1)}, bf16[512,2048]{1,0:T(8,128)(2,1)}) async-done(((bf16[512,2048]{1,0:T(8,128)(2,1)}, bf16[512,2048]{1,0:T(8,128)(2,1)}), (bf16[512,2048]{1,0:T(8,128)(2,1)}, bf16[512,2048]{1,0:T(8,128)(2,1)})) %all-reduce.3.cloned.1.call-update) | async-done | bytes 4194320 | tf_op jit(solution)/shard_map/psum | solution.py:24
  992.2 3.3 copy.26
  995.5 1.3 copy.27
  (93 shorter events, 4.7 us)
Async XLA Ops:
  7.2 10.9 %copy-start = (bf16[512,2048]{1,0:T(8,128)(2,1)S(1)}, bf16[512,2048]{1,0:T(8,128)(2,1)}, u32[]{:S(2)}) copy-start(bf16[512,2048]{1,0:T(8,128)(2,1)} %param.13) | copy-start | bytes 6291460
  7.2 7.1 copy-start.18
  7.2 8.9 copy-start.19
  7.2 59.0 %all-gather.21.cloned.1.call-start = ((), (), s32[]{:S(2)}) async-start(), calls=%async_computation.10 | async-start | bytes 1949696 | tf_op jit(solution)/shard_map/all_gather | solution.py:40
  9.1 112.8 %all-gather.19.cloned.1.call-start = ((), (), s32[]{:S(2)}) async-start(), calls=%async_computation.9 | async-start | bytes 1949696 | tf_op jit(solution)/shard_map/all_gather | solution.py:39
  10.8 166.1 %all-gather.23.cloned.1.call-start = ((), (), s32[]{:S(2)}) async-start(), calls=%async_computation.11 | async-start | bytes 1949696 | tf_op jit(solution)/shard_map/all_gather | solution.py:41
  12.5 219.8 %all-gather.15.cloned.1.call-start = ((), (), s32[]{:S(2)}) async-start(), calls=%async_computation.7 | async-start | bytes 1949696 | tf_op jit(solution)/shard_map/all_gather | solution.py:40
  13.1 274.7 %all-gather.13.cloned.1.call-start = ((), (), s32[]{:S(2)}) async-start(), calls=%async_computation.6 | async-start | bytes 1949696 | tf_op jit(solution)/shard_map/all_gather | solution.py:39
  13.7 329.0 %all-gather.17.cloned.1.call-start = ((), (), s32[]{:S(2)}) async-start(), calls=%async_computation.8 | async-start | bytes 1949696 | tf_op jit(solution)/shard_map/all_gather | solution.py:41
  14.3 410.0 %reduce-scatter.29.cloned.1.call-start = ((), (), s32[]{:S(2)}) async-start(), calls=%async_computation.17 | async-start | bytes 2228224
  176.9 4.3 copy-start.7
  180.5 0.7 copy-start.10
  187.0 319.3 %reduce-scatter.27.cloned.1.call-start = ((), (), s32[]{:S(2)}) async-start(), calls=%async_computation.16 | async-start | bytes 2228224
  189.6 42.7 %copy-start.5 = (bf16[256,2048]{1,0:T(8,128)(2,1)S(1)}, bf16[256,2048]{1,0:T(8,128)(2,1)}, u32[]{:S(2)}) copy-start(bf16[256,2048]{1,0:T(8,128)(2,1)} %gather_fusion) | copy-start | bytes 3145732
  193.9 148.7 %copy-start.6 = (bf16[256,2048]{1,0:T(8,128)(2,1)}, bf16[256,2048]{1,0:T(8,128)(2,1)S(1)}, u32[]{:S(2)}) copy-start(bf16[256,2048]{1,0:T(8,128)(2,1)S(1)} %gather_fusion.6) | copy-start | bytes 3145732
  346.0 0.7 copy-start.16
  348.7 2.5 copy-start.12
  351.2 237.1 %reduce-scatter.23.cloned.1.call-start = ((), (), s32[]{:S(2)}) async-start(), calls=%async_computation.14 | async-start | bytes 2228224
  353.2 2.6 copy-start.14
  355.8 314.3 %reduce-scatter.19.cloned.1.call-start = ((), (), s32[]{:S(2)}) async-start(), calls=%async_computation.12 | async-start | bytes 2228224
  360.2 391.8 %reduce-scatter.25.cloned.1.call-start = ((), (), s32[]{:S(2)}) async-start(), calls=%async_computation.15 | async-start | bytes 2228224
  361.1 2.7 copy-start.8
  363.6 470.3 %reduce-scatter.21.cloned.1.call-start = ((), (), s32[]{:S(2)}) async-start(), calls=%async_computation.13 | async-start | bytes 2228224
  364.5 2.7 copy-start.17
  366.9 625.3 %all-reduce.3.cloned.1.call-start = ((), (), s32[]{:S(2)}) async-start(), calls=%async_computation.18 | async-start | bytes 8388608 | tf_op jit(solution)/shard_map/psum | solution.py:24
  369.5 3.6 copy-start.15
  373.1 2.4 copy-start.4
  373.1 2.4 copy-start.13
  376.3 3.6 copy-start.11
  382.1 3.6 copy-start.9
  385.8 2.4 copy-start.3
  992.2 3.3 copy-start.2
  992.2 4.6 copy-start.1
Sparse Core Ops, SparseCore 0:
  11.2 55.0 all-gather.20
  69.3 52.4 all-gather.18
  124.4 52.4 all-gather.22
  179.8 52.4 all-gather.14
  235.3 52.4 all-gather.12
  290.2 52.4 all-gather.16
  346.9 77.3 reduce-scatter.28
  428.5 77.7 reduce-scatter.26
  510.5 77.6 reduce-scatter.22
  592.3 77.7 reduce-scatter.18
  674.3 77.7 reduce-scatter.24
  756.2 77.7 reduce-scatter.20
  837.2 154.9 all-reduce.2
where the time goes:
time: 1000 us
  waiting for transfers between devices  870 us (87%)
  local copies, waits for them, and re-layouts  65.4 us (7%)
  matrix products  39.4 us (4%)
  between operations  14.3 us (1%)
  other arithmetic  13.1 us (1%)
    unnamed x19, waiting for transfers between devices  429 us
    psum x1, waiting for transfers between devices, group_total(): return lax.psum(partial_value.astype(jnp.bfloat16), 'fsdp')  155 us
    all_gather x2, waiting for transfers between devices, body(): lax.all_gather(gate_w[expert], 'dp', axis=0, tiled=True)  105 us
    all_gather x2, waiting for transfers between devices, body(): lax.all_gather(down_w[expert], 'dp', axis=1, tiled=True)  104 us
    all_gather x2, waiting for transfers between devices, body(): lax.all_gather(up_w[expert], 'dp', axis=0, tiled=True)  77.8 us
    unnamed x54, local copies, waits for them, and re-layouts  28.4 us
  transfers between devices with their start and end apart: 13, of which 13 were waited for; matrix products, arithmetic and copies ran while one was open for 11% of the time, Pallas kernels for 0%

commit v1 on v0

--- a/solution.py
+++ b/solution.py
@@ -21,7 +21,8 @@
 
 
 def group_total(partial_value):
-    return lax.psum(partial_value.astype(jnp.bfloat16), "fsdp")
+    solve_frame = lambda arr_in: lax.all_gather(arr_in, axis_name="fsdp").sum(axis=0)
+    return solve_frame(partial_value.astype(jnp.bfloat16))
 
 
 def body(tokens, expert_ids, route_probs, gate_w, up_w, down_w, out_grad):

time: 1000 us -> 1570 us (1.57)
  waiting for transfers between devices: 870 us -> 1410 us
  other arithmetic: 13.1 us -> 39.3 us
    all_gather x0 -> x2, waiting for transfers between devices: none -> 694 us  [group_total(): lax.all_gather(arr_in, axis_name='fsdp').sum(axis=0)]
    psum x1 -> x0, waiting for transfers between devices: 155 us -> none  [group_total(): return lax.psum(partial_value.astype(jnp.bfloat16), 'fsdp')]
    reduce_sum x0 -> x2, other arithmetic: none -> 26.2 us  [group_total(): lax.all_gather(arr_in, axis_name='fsdp').sum(axis=0)]
    unnamed x19 -> x20, waiting for transfers between devices: 429 us -> 428 us
  transfers between devices with their start and end apart: 13 -> 14, of which waited for: 13 -> 14; matrix products, arithmetic and copies ran while one was open for 11% -> 8% of each run, Pallas kernels for 0% -> 0%
where the time goes in v1:
time: 1570 us; the launch traced here: 1560 us
  waiting for transfers between devices  1410 us (90%)
  local copies, waits for them, and re-layouts  60.7 us (4%)
  matrix products  39.4 us (3%)
  other arithmetic  39.3 us (3%)
    all_gather x2, waiting for transfers between devices, group_total(): lax.all_gather(arr_in, axis_name='fsdp').sum(axis=0)  694 us
    unnamed x20, waiting for transfers between devices  428 us
    all_gather x2, waiting for transfers between devices, body(): lax.all_gather(gate_w[expert], 'dp', axis=0, tiled=True)  105 us
    all_gather x2, waiting for transfers between devices, body(): lax.all_gather(down_w[expert], 'dp', axis=1, tiled=True)  104 us
    all_gather x2, waiting for transfers between devices, body(): lax.all_gather(up_w[expert], 'dp', axis=0, tiled=True)  77.8 us
  transfers between devices with their start and end apart: 14, of which 14 were waited for; matrix products, arithmetic and copies ran while one was open for 8% of the time, Pallas kernels for 0%

profile of v1, /device:TPU:4, one launch (start us, length us, event | category | flops | bytes accessed | tf_op | source)
XLA Modules:
  0.0 1564.2 jit_solution(10778134750302694187)
XLA Ops:
  7.2 1.8 fusion.32
  9.1 1.7 fusion.31
  10.8 1.7 fusion.30
  16.1 1.9 gather_fusion.4
  18.1 1.4 gather_fusion.3
  19.4 5.2 gather_fusion.8
  24.6 41.6 %all-gather.25.cloned.1.call-done = bf16[1,2048,448]{1,2,0:T(8,128)(2,1)} async-done(((bf16[1,128,448]{1,2,0:T(8,128)(2,1)}), bf16[1,2048,448]{1,2,0:T(8,128)(2,1)}) %all-gather.25.cloned.1.call-update) | async-done | bytes 1835024 | tf_op jit(solution)/shard_map/all_gather | solution.py:41
  66.2 3.1 fusion.8
  69.3 52.5 %all-gather.23.cloned.1.call-done = bf16[1,2048,448]{1,2,0:T(8,128)(2,1)} async-done(((bf16[1,128,448]{1,2,0:T(8,128)(2,1)}), bf16[1,2048,448]{1,2,0:T(8,128)(2,1)}) %all-gather.23.cloned.1.call-update) | async-done | bytes 1835024 | tf_op jit(solution)/shard_map/all_gather | solution.py:40
  121.8 3.0 fusion.12
  124.9 52.0 %all-gather.27.cloned.1.call-done = bf16[1,448,2048]{2,1,0:T(8,128)(2,1)} async-done(((bf16[1,448,128]{2,1,0:T(8,128)(2,1)}), bf16[1,448,2048]{2,1,0:T(8,128)(2,1)}) %all-gather.27.cloned.1.call-update) | async-done | bytes 1835024 | tf_op jit(solution)/shard_map/all_gather | solution.py:42
  176.9 3.7 multiply_convert_fusion.2
  181.2 2.0 convolution_convert_fusion.4
  183.2 3.8 copy.22
  187.3 2.3 gather_fusion
  189.6 4.3 gather_fusion.6
  194.1 1.9 gather_fusion.1
  196.1 36.2 %all-gather.19.cloned.1.call-done = bf16[1,2048,448]{1,2,0:T(8,128)(2,1)} async-done(((bf16[1,128,448]{1,2,0:T(8,128)(2,1)}), bf16[1,2048,448]{1,2,0:T(8,128)(2,1)}) %all-gather.19.cloned.1.call-update) | async-done | bytes 1835024 | tf_op jit(solution)/shard_map/all_gather | solution.py:41
  232.3 3.0 fusion.18
  235.4 52.4 %all-gather.17.cloned.1.call-done = bf16[1,2048,448]{1,2,0:T(8,128)(2,1)} async-done(((bf16[1,128,448]{1,2,0:T(8,128)(2,1)}), bf16[1,2048,448]{1,2,0:T(8,128)(2,1)}) %all-gather.17.cloned.1.call-update) | async-done | bytes 1835024 | tf_op jit(solution)/shard_map/all_gather | solution.py:40
  287.8 3.1 fusion.22
  290.8 51.8 %all-gather.21.cloned.1.call-done = bf16[1,448,2048]{2,1,0:T(8,128)(2,1)} async-done(((bf16[1,448,128]{2,1,0:T(8,128)(2,1)}), bf16[1,448,2048]{2,1,0:T(8,128)(2,1)}) %all-gather.21.cloned.1.call-update) | async-done | bytes 1835024 | tf_op jit(solution)/shard_map/all_gather | solution.py:42
  342.7 3.3 multiply_convert_fusion.4
  346.0 0.7 copy-done.15
  346.7 2.0 convolution_convert_fusion.5
  348.7 2.5 copy.20
  351.2 2.0 convolution_convert_fusion.1
  353.2 2.5 copy.16
  355.8 2.0 convolution_convert_fusion.3
  357.8 2.4 copy.12
  360.3 0.8 convolution_convert_fusion
  361.0 2.5 copy.18
  363.7 0.8 convolution_convert_fusion.2
  364.4 2.4 copy.14
  367.2 2.3 convolution_multiply_fusion.1
  369.5 3.6 gather_fusion.2
  373.1 2.4 fusion.20
  375.5 0.7 convolution_add_fusion.1
  376.2 3.6 gather_fusion.7
  379.9 2.2 convolution_multiply_fusion
  382.1 3.6 gather_fusion.5
  385.7 2.4 fusion.10
  388.1 0.7 convolution_add_fusion
  388.8 3.6 gather_fusion.9
  392.4 9.4 fusion.1
  402.4 21.9 %reduce-scatter.29.cloned.1.call-done = bf16[128,448]{1,0:T(8,128)(2,1)} async-done(((bf16[2048,448]{1,0:T(8,128)(2,1)}), bf16[128,448]{1,0:T(8,128)(2,1)}) %reduce-scatter.29.cloned.1.call-update) | async-done | bytes 114704
  424.3 1.0 copy.23
  425.3 80.9 %reduce-scatter.27.cloned.1.call-done = bf16[128,448]{1,0:T(8,128)(2,1)} async-done(((bf16[2048,448]{1,0:T(8,128)(2,1)}), bf16[128,448]{1,0:T(8,128)(2,1)}) %reduce-scatter.27.cloned.1.call-update) | async-done | bytes 114704
  506.2 1.0 copy.21
  507.3 81.0 %reduce-scatter.23.cloned.1.call-done = bf16[128,448]{1,0:T(8,128)(2,1)} async-done(((bf16[2048,448]{1,0:T(8,128)(2,1)}), bf16[128,448]{1,0:T(8,128)(2,1)}) %reduce-scatter.23.cloned.1.call-update) | async-done | bytes 114704
  588.2 1.0 copy.17
  589.3 80.7 %reduce-scatter.19.cloned.1.call-done = bf16[128,448]{1,0:T(8,128)(2,1)} async-done(((bf16[2048,448]{1,0:T(8,128)(2,1)}), bf16[128,448]{1,0:T(8,128)(2,1)}) %reduce-scatter.19.cloned.1.call-update) | async-done | bytes 114704
  670.0 1.0 copy.13
  671.0 80.9 %reduce-scatter.25.cloned.1.call-done = bf16[128,448]{1,0:T(8,128)(2,1)} async-done(((bf16[2048,448]{1,0:T(8,128)(2,1)}), bf16[128,448]{1,0:T(8,128)(2,1)}) %reduce-scatter.25.cloned.1.call-update) | async-done | bytes 114704
  752.0 1.0 copy.19
  753.0 80.8 %reduce-scatter.21.cloned.1.call-done = bf16[128,448]{1,0:T(8,128)(2,1)} async-done(((bf16[2048,448]{1,0:T(8,128)(2,1)}), bf16[128,448]{1,0:T(8,128)(2,1)}) %reduce-scatter.21.cloned.1.call-update) | async-done | bytes 114704
  833.8 1.0 copy.15
  834.8 0.7 pad_maximum_fusion.2
  835.6 0.7 pad_maximum_fusion.1
  836.3 0.7 pad_maximum_fusion
  837.0 353.7 %all-gather.31.cloned.1.call-done = bf16[8192,2048]{1,0:T(8,128)(2,1)} async-done(((bf16[512,2048]{1,0:T(8,128)(2,1)}), bf16[8192,2048]{1,0:T(8,128)(2,1)}) %all-gather.31.cloned.1.call-update) | async-done | bytes 33554448 | tf_op jit(solution)/shard_map/all_gather | solution.py:24
  1190.7 13.1 reduce_sum.65
  1203.7 340.7 %all-gather.29.cloned.1.call-done = bf16[8192,2048]{1,0:T(8,128)(2,1)} async-done(((bf16[512,2048]{1,0:T(8,128)(2,1)}), bf16[8192,2048]{1,0:T(8,128)(2,1)}) %all-gather.29.cloned.1.call-update) | async-done | bytes 33554448 | tf_op jit(solution)/shard_map/all_gather | solution.py:24
  1544.4 13.2 reduce_sum.64
  (94 shorter events, 6.0 us)
Async XLA Ops:
  7.2 10.9 copy-start
  7.2 7.1 copy-start.17
  7.2 8.9 copy-start.18
  7.2 59.0 %all-gather.25.cloned.1.call-start = ((), (), s32[]{:S(2)}) async-start(), calls=%async_computation.10 | async-start | bytes 1949696 | tf_op jit(solution)/shard_map/all_gather | solution.py:41
  9.1 112.8 %all-gather.23.cloned.1.call-start = ((), (), s32[]{:S(2)}) async-start(), calls=%async_computation.9 | async-start | bytes 1949696 | tf_op jit(solution)/shard_map/all_gather | solution.py:40
  10.8 166.1 %all-gather.27.cloned.1.call-start = ((), (), s32[]{:S(2)}) async-start(), calls=%async_computation.11 | async-start | bytes 1949696 | tf_op jit(solution)/shard_map/all_gather | solution.py:42
  12.5 219.8 %all-gather.19.cloned.1.call-start = ((), (), s32[]{:S(2)}) async-start(), calls=%async_computation.7 | async-start | bytes 1949696 | tf_op jit(solution)/shard_map/all_gather | solution.py:41
  13.1 274.7 %all-gather.17.cloned.1.call-start = ((), (), s32[]{:S(2)}) async-start(), calls=%async_computation.6 | async-start | bytes 1949696 | tf_op jit(solution)/shard_map/all_gather | solution.py:40
  13.7 329.0 %all-gather.21.cloned.1.call-start = ((), (), s32[]{:S(2)}) async-start(), calls=%async_computation.8 | async-start | bytes 1949696 | tf_op jit(solution)/shard_map/all_gather | solution.py:42
  14.3 410.0 %reduce-scatter.29.cloned.1.call-start = ((), (), s32[]{:S(2)}) async-start(), calls=%async_computation.19 | async-start | bytes 2228224
  176.9 4.3 copy-start.6
  180.5 0.7 copy-start.9
  187.0 319.2 %reduce-scatter.27.cloned.1.call-start = ((), (), s32[]{:S(2)}) async-start(), calls=%async_computation.18 | async-start | bytes 2228224
  189.6 42.7 %copy-start.4 = (bf16[256,2048]{1,0:T(8,128)(2,1)S(1)}, bf16[256,2048]{1,0:T(8,128)(2,1)}, u32[]{:S(2)}) copy-start(bf16[256,2048]{1,0:T(8,128)(2,1)} %gather_fusion) | copy-start | bytes 3145732
  193.9 148.7 %copy-start.5 = (bf16[256,2048]{1,0:T(8,128)(2,1)}, bf16[256,2048]{1,0:T(8,128)(2,1)S(1)}, u32[]{:S(2)}) copy-start(bf16[256,2048]{1,0:T(8,128)(2,1)S(1)} %gather_fusion.6) | copy-start | bytes 3145732
  346.0 0.7 copy-start.15
  348.7 2.5 copy-start.11
  351.2 237.0 %reduce-scatter.23.cloned.1.call-start = ((), (), s32[]{:S(2)}) async-start(), calls=%async_computation.16 | async-start | bytes 2228224
  353.2 2.5 copy-start.13
  355.7 314.3 %reduce-scatter.19.cloned.1.call-start = ((), (), s32[]{:S(2)}) async-start(), calls=%async_computation.14 | async-start | bytes 2228224
  360.2 391.7 %reduce-scatter.25.cloned.1.call-start = ((), (), s32[]{:S(2)}) async-start(), calls=%async_computation.17 | async-start | bytes 2228224
  361.0 2.6 copy-start.7
  363.6 470.2 %reduce-scatter.21.cloned.1.call-start = ((), (), s32[]{:S(2)}) async-start(), calls=%async_computation.15 | async-start | bytes 2228224
  364.4 2.8 copy-start.16
  366.9 823.8 %all-gather.31.cloned.1.call-start = ((), (), s32[]{:S(2)}) async-start(), calls=%async_computation.13 | async-start | bytes 35651584 | tf_op jit(solution)/shard_map/all_gather | solution.py:24
  369.5 3.6 copy-start.14
  373.1 2.4 copy-start.3
  373.1 2.4 copy-start.12
  376.2 3.6 copy-start.10
  382.1 3.6 copy-start.8
  385.7 2.4 copy-start.2
  401.8 1142.6 %all-gather.29.cloned.1.call-start = ((), (), s32[]{:S(2)}) async-start(), calls=%async_computation.12 | async-start | bytes 35651584 | tf_op jit(solution)/shard_map/all_gather | solution.py:24
  1544.4 13.2 copy-start.1
Sparse Core Ops, SparseCore 0:
  11.2 55.0 all-gather.24
  69.3 52.4 all-gather.22
  124.4 52.4 all-gather.26
  179.8 52.4 all-gather.18
  235.3 52.4 all-gather.16
  290.2 52.4 all-gather.20
  346.9 77.3 reduce-scatter.28
  428.5 77.6 reduce-scatter.26
  510.5 77.7 reduce-scatter.22
  592.3 77.6 reduce-scatter.18
  674.2 77.6 reduce-scatter.24
  756.0 77.7 reduce-scatter.20
  836.2 354.4 all-gather.30
  1192.9 351.4 all-gather.28
